TPU v7x, 32 devices: a whole 2x2x4 slice. The times are simulated.
32 devices in a mesh: cuts: 2 (over x), mode: 8 (over z, y), branch: 2 (over core).
Axes of the slice: x: 2, y: 2, z: 4, core: 2. Of those that a mesh axis runs over, the one named last changes fastest.
Arguments:
- leaves: bfloat16 [8, 2, 32, 512, 512], P('branch', None, ('cuts', 'mode')), parts along dimension 2, may hold values from -0.1875 to 0.1875
- join_order: int32 [7], replicated, may hold values from 0 to 1
- slice_values: int32 [32], P(('cuts', 'mode')), parts along dimension 0, may hold values from 0 to 1
- boundary: bfloat16 [2, 2, 512, 512], replicated, may hold values from -4 to 4
Outputs:
- amplitudes: float32 [2, 32, 512, 512], P(None, ('cuts', 'mode'), 'branch'), parts along dimension 1
There are 2 independent parts, one for each index of `cuts`. A program takes and returns all parts, laid end to end along the dimension named above; an argument that names none is the same for every part. Nothing has to cross between parts.
Inputs may be any that keep to these rules, and one draw needn't show every extreme that they name: `join_order`: 1 puts the second operand of the join on the left.
All inputs are finite; a program needn't handle non-finite values.
Results may differ from a plain program's by a relative error of at most 0.0076.
Values may be sent and summed in bfloat16 or wider, within the bound.
A program may use at most 64 MiB of HBM per device.

v0:
```python
import jax
import jax.numpy as jnp
from jax import lax
from jax.sharding import PartitionSpec as P


def from_partner(value, axis, bit):
    mask = 2**bit
    pairs = [(source, source ^ mask) for source in range(lax.axis_size(axis))]
    return lax.ppermute(value, axis, pairs)


def complex_sums(left_op, right_op):
    spec = "bij,bjk->bik"
    real_part = jnp.einsum(
        spec, left_op[0], right_op[0], preferred_element_type=jnp.float32
    ) - jnp.einsum(spec, left_op[1], right_op[1], preferred_element_type=jnp.float32)
    imag_part = jnp.einsum(
        spec, left_op[0], right_op[1], preferred_element_type=jnp.float32
    ) + jnp.einsum(spec, left_op[1], right_op[0], preferred_element_type=jnp.float32)
    return jnp.stack([real_part, imag_part])


def complex_product(left_op, right_op):
    return complex_sums(left_op, right_op).astype(jnp.bfloat16)


def join_pair(left_op, right_op, swapped):
    return lax.cond(
        swapped == 1,
        lambda: complex_product(right_op, left_op),
        lambda: complex_product(left_op, right_op),
    )


def split_rows(tensor, blocks):
    shape = tensor.shape
    return tensor.reshape(shape[0], shape[1], blocks, shape[2] // blocks, shape[3])


def merge_rows(tensor):
    shape = tensor.shape
    width = shape[4]
    total_rows = shape[1] * shape[2] * shape[3]
    return tensor.reshape(shape[0], total_rows // width, width, width)


def per_device(leaves, join_order, slice_values, boundary):
    blocks = lax.axis_size("mode")
    branch_index = lax.axis_index("branch")
    base_index = 2 * branch_index
    first_pair = join_pair(leaves[0], leaves[1], join_order[base_index])
    second_pair = join_pair(leaves[2], leaves[3], join_order[base_index + 1])
    first_pair, second_pair = (
        lax.all_to_all(
            split_rows(first_pair, blocks), "mode", split_axis=2, concat_axis=1, tiled=True
        ),
        lax.all_to_all(
            split_rows(second_pair, blocks), "mode", split_axis=2, concat_axis=1, tiled=True
        ),
    )
    first_pair = merge_rows(first_pair)
    second_pair = merge_rows(second_pair)
    middle = join_pair(first_pair, second_pair, join_order[4 + branch_index])
    middle = merge_rows(
        lax.all_to_all(split_rows(middle, blocks), "mode", split_axis=2, concat_axis=1, tiled=True)
    )
    width = middle.shape[3]
    half_rows = width // 2
    chosen = jnp.where(
        slice_values[None, :, None, None] == 1, boundary[1][:, None], boundary[0][:, None]
    )
    top_order = join_order[-1]
    partner = from_partner(middle, "branch", 0)
    is_first = branch_index == 0
    upper = jnp.where(is_first, middle, partner)
    lower = jnp.where(is_first, partner, middle)
    leading = jnp.where(top_order == 1, lower, upper)
    trailing = jnp.where(top_order == 1, upper, lower)
    leading = lax.dynamic_slice_in_dim(leading, branch_index * half_rows, half_rows, 2)
    top_half = complex_product(leading, trailing)
    amplitudes = complex_sums(top_half, chosen)
    return amplitudes


def solution(mesh):
    in_specs = (P("branch", None, ("cuts", "mode"), None, None), P(), P(("cuts", "mode")), P())
    out_specs = P(None, ("cuts", "mode"), "branch", None)
    return jax.shard_map(
        per_device, mesh=mesh, in_specs=in_specs, out_specs=out_specs, check_vma=False
    )
```

profile of v0, /device:TPU:0, one launch (start us, length us, event | category | flops | bytes accessed | tf_op | source)
XLA Modules:
  0.0 195.7 jit_solution(156778789101351986)
XLA Ops:
  0.0 5.7 %slice_bitcast_fusion = (bf16[2,2,512,512]{3,2,1,0:T(8,128)(2,1)}, bf16[2,2,512,512]{3,2,1,0:T(8,128)(2,1)S(1)}, bf16[2,2,512,512]{3,2,1,0:T(8,128)(2,1)}, bf16[2,2,512,512]{3,2,1,0:T(8,128)(2,1)}) fusion(bf16[4,2,2,512,512]{4,3,2,1,0:T(8,128)(2,1)} %param.10), kind=kLoop, calls=%fused_computation.127 | loop fusion | bytes 16777216 | tf_op jit(solution)/shard_map/squeeze | solution.py:53
  7.0 6.6 %conditional.7 = (bf16[2,2,512,512]{3,2,1,0:T(8,128)(2,1)}) conditional(s32[]{:T(128)} %bitcast.45, (bf16[2,2,512,512]{3,2,1,0:T(8,128)(2,1)}, bf16[2,2,512,512]{3,2,1,0:T(8,128)(2,1)}) %tuple.34, (bf16[2,2,512,512]{3,2,1,0:T(8,128)(2,1)}, bf16[2,2,512,512]{3,2,1,0:T(8,128)(2,1)}) %tuple.35), branch_computations={%region_2.0_spmd, %region_3.0_spmd} | conditional | flops 2150629376 | bytes 39845952
  7.1 2.4 %fusion.36 = f32[2,512,512]{2,1,0:T(8,128)S(1)} fusion(bf16[2,2,512,512]{3,2,1,0:T(8,128)(2,1)} %get-tuple-element.49, bf16[2,2,512,512]{3,2,1,0:T(8,128)(2,1)} %get-tuple-element.48), kind=kOutput, calls=%fused_computation.45 | convolution fusion | flops 536870912 | bytes 4194304 | tf_op jit(solution)/shard_map/cond/branch_0_fun/bij,bjk->bik/dot_general | solution.py:18
  11.3 0.7 subtract_bitcast_fusion.2
  12.1 1.6 pad_maximum_fusion.2
  13.6 3.2 %copy.11 = bf16[2,2,8,64,512]{4,3,1,0,2:T(8,128)(2,1)} copy(bf16[2,2,8,64,512]{4,3,2,1,0:T(8,128)(2,1)} %bitcast.213) | data formatting | bytes 4194304 | tf_op jit(solution)/shard_map/reshape | solution.py:38
  16.8 7.3 %all-to-all-start.1 = ((bf16[2,2,8,64,512]{4,3,1,0,2:T(8,128)(2,1)}), bf16[2,2,8,64,512]{4,3,1,0,2:T(8,128)(2,1)}, u32[]{:S(2)}, u32[]{:S(2)}) async-start(bf16[2,2,8,64,512]{4,3,1,0,2:T(8,128)(2,1)} %copy.11), calls=%async_computation.1 | async-start | bytes 4194304 | tf_op jit(solution)/shard_map/all_to_all | solution.py:58
  24.7 4.5 %conditional.6 = (bf16[2,2,512,512]{3,2,1,0:T(8,128)(2,1)S(1)}) conditional(s32[]{:T(128)} %bitcast.38, (bf16[2,2,512,512]{3,2,1,0:T(8,128)(2,1)}, bf16[2,2,512,512]{3,2,1,0:T(8,128)(2,1)S(1)}) %tuple.32, (bf16[2,2,512,512]{3,2,1,0:T(8,128)(2,1)S(1)}, bf16[2,2,512,512]{3,2,1,0:T(8,128)(2,1)}) %tuple.33), branch_computations={%region_0.0_spmd, %region_1.0_spmd} | conditional | flops 2150629376 | bytes 31457316
  24.8 2.1 %fusion.18 = f32[2,512,512]{2,1,0:T(8,128)S(1)} fusion(bf16[2,2,512,512]{3,2,1,0:T(8,128)(2,1)} %get-tuple-element.47, bf16[2,2,512,512]{3,2,1,0:T(8,128)(2,1)S(1)} %get-tuple-element.46), kind=kOutput, calls=%fused_computation.24 | convolution fusion | flops 536870912 | bytes 4194304 | tf_op jit(solution)/shard_map/cond/branch_1_fun/bij,bjk->bik/dot_general | solution.py:18
  28.3 0.7 subtract_bitcast_fusion.1
  29.2 1.5 copy.9
  30.7 41.7 %all-to-all-done.1 = bf16[2,2,8,64,512]{4,3,1,0,2:T(8,128)(2,1)} async-done(((bf16[2,2,8,64,512]{4,3,1,0,2:T(8,128)(2,1)}), bf16[2,2,8,64,512]{4,3,1,0,2:T(8,128)(2,1)}, u32[]{:S(2)}, u32[]{:S(2)}) %all-to-all-start.1) | async-done | bytes 2097184 | tf_op jit(solution)/shard_map/all_to_all | solution.py:58
  72.4 4.4 %all-to-all-start = ((bf16[2,2,8,64,512]{4,3,1,0,2:T(8,128)(2,1)}), bf16[2,2,8,64,512]{4,3,1,0,2:T(8,128)(2,1)}, u32[]{:S(2)}, u32[]{:S(2)}) async-start(bf16[2,2,8,64,512]{4,3,1,0,2:T(8,128)(2,1)} %copy.9), calls=%async_computation | async-start | bytes 4194304 | tf_op jit(solution)/shard_map/all_to_all | solution.py:55
  77.5 1.8 copy.12
  79.3 45.3 %all-to-all-done = bf16[2,2,8,64,512]{4,3,1,0,2:T(8,128)(2,1)} async-done(((bf16[2,2,8,64,512]{4,3,1,0,2:T(8,128)(2,1)}), bf16[2,2,8,64,512]{4,3,1,0,2:T(8,128)(2,1)}, u32[]{:S(2)}, u32[]{:S(2)}) %all-to-all-start) | async-done | bytes 2097184 | tf_op jit(solution)/shard_map/all_to_all | solution.py:55
  124.6 1.8 copy.10
  126.4 3.3 %conditional.8 = (bf16[2,2,512,512]{3,2,1,0:T(8,128)(2,1)S(1)}) conditional(s32[]{:T(128)} %bitcast.37, (bf16[2,2,512,512]{3,2,1,0:T(8,128)(2,1)S(1)}, bf16[2,2,512,512]{3,2,1,0:T(8,128)(2,1)S(1)}) %tuple.55, (bf16[2,2,512,512]{3,2,1,0:T(8,128)(2,1)S(1)}, bf16[2,2,512,512]{3,2,1,0:T(8,128)(2,1)S(1)}) %tuple.56), branch_computations={%region_4.0_spmd, %region_5.0_spmd} | conditional | flops 2150629376 | bytes 23068680
  127.2 0.7 add_bitcast_fusion.4
  129.9 51.8 %all_to_all.45 = bf16[2,2,8,64,512]{4,3,1,0,2:T(8,128)(2,1)S(1)} all-to-all(bf16[2,2,8,64,512]{4,3,1,0,2:T(8,128)(2,1)S(1)} %copy.13), channel_id=1, replica_groups=mesh['cuts'=2,'mode'=8,'branch'=2] {'mode'}, dimensions={2} | all-to-all | bytes 4194304 | tf_op jit(solution)/shard_map/all_to_all | solution.py:66
  181.7 1.5 copy.14
  183.9 1.7 slice_bitcast_fusion.9
  185.9 1.9 collective-permute-done
  187.8 2.6 %broadcast_select_fusion.3 = (bf16[2,2,512,512]{3,2,1,0:T(8,128)(2,1)S(1)}, bf16[2,2,512,512]{3,2,1,0:T(8,128)(2,1)S(1)}, bf16[2,2,512,512]{3,2,1,0:T(8,128)(2,1)S(1)}) fusion(pred[]{:T(512)} %bitcast.36, bf16[2,2,512,512]{3,2,1,0:T(8,128)(2,1)} %collective-permute-done, bf16[2,2,512,512]{3,2,1,0:T(8,128)(2,1)} %bitcast.59, pred[]{:T(512)S(6)} %eq.28), kind=kLoop, calls=%fused_computation.134 | loop fusion | flops 3145728 | bytes 10485762 | tf_op jit(solution)/shard_map/jit(_where)/select_n | solution.py:79
  194.2 1.5 pad_maximum_fusion.6
  (33 shorter events, 10.7 us)
Async XLA Ops:
  0.0 5.7 %copy-start.6 = (s32[7]{0:T(128)S(1)}, s32[7]{0:T(128)}, u32[]{:S(2)}) copy-start(s32[7]{0:T(128)} %param.11) | copy-start | bytes 88
  7.0 2.4 %copy-start.2 = (bf16[2,2,512,512]{3,2,1,0:T(8,128)(2,1)S(1)}, bf16[2,2,512,512]{3,2,1,0:T(8,128)(2,1)}, u32[]{:S(2)}) copy-start(bf16[2,2,512,512]{3,2,1,0:T(8,128)(2,1)} %get-tuple-element.49) | copy-start | bytes 6291460 | tf_op jit(solution)/shard_map/conditional.1
  7.1 2.8 %copy-start.4 = (bf16[2,2,512,512]{3,2,1,0:T(8,128)(2,1)S(1)}, bf16[2,2,512,512]{3,2,1,0:T(8,128)(2,1)}, u32[]{:S(2)}) copy-start(bf16[2,2,512,512]{3,2,1,0:T(8,128)(2,1)} %get-tuple-element.48) | copy-start | bytes 6291460 | tf_op jit(solution)/shard_map/conditional.1
  16.8 55.7 %all-to-all-start.1 = ((bf16[2,2,8,64,512]{4,3,1,0,2:T(8,128)(2,1)}), bf16[2,2,8,64,512]{4,3,1,0,2:T(8,128)(2,1)}, u32[]{:S(2)}, u32[]{:S(2)}) async-start(bf16[2,2,8,64,512]{4,3,1,0,2:T(8,128)(2,1)} %copy.11), calls=%async_computation.1 | async-start | bytes 4194304 | tf_op jit(solution)/shard_map/all_to_all | solution.py:58
  24.8 2.1 %copy-start.1 = (bf16[2,2,512,512]{3,2,1,0:T(8,128)(2,1)S(1)}, bf16[2,2,512,512]{3,2,1,0:T(8,128)(2,1)}, u32[]{:S(2)}) copy-start(bf16[2,2,512,512]{3,2,1,0:T(8,128)(2,1)} %get-tuple-element.47) | copy-start | bytes 6291460 | tf_op jit(solution)/shard_map/conditional
  72.4 52.2 %all-to-all-start = ((bf16[2,2,8,64,512]{4,3,1,0,2:T(8,128)(2,1)}), bf16[2,2,8,64,512]{4,3,1,0,2:T(8,128)(2,1)}, u32[]{:S(2)}, u32[]{:S(2)}) async-start(bf16[2,2,8,64,512]{4,3,1,0,2:T(8,128)(2,1)} %copy.9), calls=%async_computation | async-start | bytes 4194304 | tf_op jit(solution)/shard_map/all_to_all | solution.py:55
  181.7 2.2 %copy-start.7 = (s32[2]{0:T(128)S(1)}, s32[2]{0:T(128)}, u32[]{:S(2)}) copy-start(s32[2]{0:T(128)} %param.12) | copy-start | bytes 28
  183.3 4.5 %collective-permute-start = (bf16[2,2,512,512]{3,2,1,0:T(8,128)(2,1)}, bf16[2,2,512,512]{3,2,1,0:T(8,128)(2,1)}, u32[]{:S(2)}, u32[]{:S(2)}) collective-permute-start(bf16[2,2,512,512]{3,2,1,0:T(8,128)(2,1)} %bitcast.59), channel_id=1, source_target_pairs={{0,1},{1,0},{2,3},{3,2},{4,5},{5,4},{6,7},{7,6},{8,9},{9,8},{10,11... | collective-permute-start | bytes 6291464 | tf_op jit(solution)/shard_map/ppermute | solution.py:10
where the time goes:
time: 196 us
  waiting for transfers between devices  88.9 us (45%)
  blocking collectives  51.8 us (26%)
  local copies, waits for them, and re-layouts  18.6 us (9%)
  matrix products  15.1 us (8%)
  starting transfers between devices  11.7 us (6%)
  other arithmetic  6.63 us (3%)
  between operations  2.74 us (1%)
    all_to_all x1, blocking collectives, per_device(): lax.all_to_all(split_rows(middle, blocks), 'mode', split_axis=2, concat_a...  51.8 us
    all_to_all x1, waiting for transfers between devices, per_device(): lax.all_to_all(split_rows(first_pair, blocks), 'mode', split_axis=2, conc...  45.3 us
    all_to_all x1, waiting for transfers between devices, per_device(): lax.all_to_all(split_rows(second_pair, blocks), 'mode', split_axis=2, con...  41.7 us
    all_to_all x1, starting transfers between devices, per_device(): lax.all_to_all(split_rows(second_pair, blocks), 'mode', split_axis=2, con...  7.31 us
    dot_general x5, matrix products, complex_sums(): jnp.einsum(spec, left_op[0], right_op[1], preferred_element_type=jnp.floa...  6.06 us
    squeeze x1, local copies, waits for them, and re-layouts, per_device(): second_pair = join_pair(leaves[2], leaves[3], join_order[base_index + 1])  5.73 us
    reshape x3, local copies, waits for them, and re-layouts, split_rows(): tensor.reshape(shape[0], shape[1], blocks, shape[2] // blocks, shape[3])  4.91 us
    all_to_all x1, starting transfers between devices, per_device(): lax.all_to_all(split_rows(first_pair, blocks), 'mode', split_axis=2, conc...  4.35 us
  transfers between devices with their start and end apart: 3, of which 3 were waited for; matrix products, arithmetic and copies ran while one was open for 5% of the time, Pallas kernels for 0%

commit v1 on v0

--- a/solution.py
+++ b/solution.py
@@ -2,6 +2,22 @@
 import jax.numpy as jnp
 from jax import lax
 from jax.sharding import PartitionSpec as P
+
+
+def exchange_in_pairs(shard, axis, split, join):
+    ways, here = (lax.axis_size(axis), lax.axis_index(axis))
+    width = shard.shape[split] // ways
+    shape = list(shard.shape)
+    shape[split] = width
+    height = shape[join]
+    shape[join] = height * ways
+    full = jnp.zeros(shape, shard.dtype)
+    for mask in range(ways):
+        part = lax.dynamic_slice_in_dim(shard, (here ^ mask) * width, width, axis=split)
+        if mask:
+            part = lax.ppermute(part, axis, [(d, d ^ mask) for d in range(ways)])
+        full = lax.dynamic_update_slice_in_dim(full, part, (here ^ mask) * height, axis=join)
+    return full
 
 
 def from_partner(value, axis, bit):
@@ -52,9 +68,7 @@
     first_pair = join_pair(leaves[0], leaves[1], join_order[base_index])
     second_pair = join_pair(leaves[2], leaves[3], join_order[base_index + 1])
     first_pair, second_pair = (
-        lax.all_to_all(
-            split_rows(first_pair, blocks), "mode", split_axis=2, concat_axis=1, tiled=True
-        ),
+        exchange_in_pairs(split_rows(first_pair, blocks), "mode", 2, 1),
         lax.all_to_all(
             split_rows(second_pair, blocks), "mode", split_axis=2, concat_axis=1, tiled=True
         ),

time: 196 us -> 188 us (0.959)
  waiting for transfers between devices: 88.9 us -> 56.1 us
  starting transfers between devices: 11.7 us -> 28.3 us
  blocking collectives: 51.8 us -> 61 us
    ppermute x0 -> x7, waiting for transfers between devices: none -> 54.4 us  [exchange_in_pairs(): part = lax.ppermute(part, axis, [(d, d ^ mask) for d in range(ways)])]
    all_to_all x1 -> x0, waiting for transfers between devices: 45.3 us -> none  [per_device(): lax.all_to_all(split_rows(first_pair, blocks), 'mode', split_axis=2, conc...]
    all_to_all x1, waiting for transfers between devices: 41.7 us -> 0.01 us  [per_device(): lax.all_to_all(split_rows(second_pair, blocks), 'mode', split_axis=2, con...]
    ppermute x0 -> x7, starting transfers between devices: none -> 21 us  [exchange_in_pairs(): part = lax.ppermute(part, axis, [(d, d ^ mask) for d in range(ways)])]
    all_to_all x1, blocking collectives: 51.8 us -> 61 us  [per_device(): lax.all_to_all(split_rows(middle, blocks), 'mode', split_axis=2, concat_a...]
    all_to_all x1 -> x0, starting transfers between devices: 4.35 us -> none  [per_device(): lax.all_to_all(split_rows(first_pair, blocks), 'mode', split_axis=2, conc...]
    reshape x3 -> x2, local copies, waits for them, and re-layouts: 4.91 us -> 3.38 us  [split_rows(): tensor.reshape(shape[0], shape[1], blocks, shape[2] // blocks, shape[3])]
  transfers between devices with their start and end apart: 3 -> 9, of which waited for: 3 -> 6; matrix products, arithmetic and copies ran while one was open for 5% -> 5% of each run, Pallas kernels for 0% -> 0%
where the time goes in v1:
time: 188 us
  blocking collectives  61 us (32%)
  waiting for transfers between devices  56.1 us (30%)
  starting transfers between devices  28.3 us (15%)
  local copies, waits for them, and re-layouts  18.3 us (10%)
  matrix products  15.1 us (8%)
  other arithmetic  5.95 us (3%)
  between operations  2.81 us (1%)
    all_to_all x1, blocking collectives, per_device(): lax.all_to_all(split_rows(middle, blocks), 'mode', split_axis=2, concat_a...  61 us
    ppermute x7, waiting for transfers between devices, exchange_in_pairs(): part = lax.ppermute(part, axis, [(d, d ^ mask) for d in range(ways)])  54.4 us
    ppermute x7, starting transfers between devices, exchange_in_pairs(): part = lax.ppermute(part, axis, [(d, d ^ mask) for d in range(ways)])  21 us
    all_to_all x1, starting transfers between devices, per_device(): lax.all_to_all(split_rows(second_pair, blocks), 'mode', split_axis=2, con...  7.31 us
    squeeze x1, local copies, waits for them, and re-layouts, per_device(): second_pair = join_pair(leaves[2], leaves[3], join_order[base_index + 1])  5.69 us
    dot_general x5, matrix products, complex_sums(): jnp.einsum(spec, left_op[0], right_op[1], preferred_element_type=jnp.floa...  4.68 us
    dot_general x5, matrix products, complex_sums(): jnp.einsum(spec, left_op[0], right_op[0], preferred_element_type=jnp.floa...  4.37 us
  transfers between devices with their start and end apart: 9, of which 6 were waited for; matrix products, arithmetic and copies ran while one was open for 5% of the time, Pallas kernels for 0%

profile of v1, /device:TPU:0, one launch (start us, length us, event | category | flops | bytes accessed | tf_op | source)
XLA Modules:
  0.0 187.7 jit_solution(138357391221148489)
XLA Ops:
  0.0 5.7 %slice_bitcast_fusion = (bf16[2,2,512,512]{3,2,1,0:T(8,128)(2,1)}, bf16[2,2,512,512]{3,2,1,0:T(8,128)(2,1)S(1)}, bf16[2,2,512,512]{3,2,1,0:T(8,128)(2,1)}, bf16[2,2,512,512]{3,2,1,0:T(8,128)(2,1)}) fusion(bf16[4,2,2,512,512]{4,3,2,1,0:T(8,128)(2,1)} %param.10), kind=kLoop, calls=%fused_computation.127 | loop fusion | bytes 16777216 | tf_op jit(solution)/shard_map/squeeze | solution.py:69
  7.0 6.5 %conditional.8 = (bf16[2,2,512,512]{3,2,1,0:T(8,128)(2,1)}) conditional(s32[]{:T(128)} %bitcast.50, (bf16[2,2,512,512]{3,2,1,0:T(8,128)(2,1)}, bf16[2,2,512,512]{3,2,1,0:T(8,128)(2,1)}) %tuple.41, (bf16[2,2,512,512]{3,2,1,0:T(8,128)(2,1)}, bf16[2,2,512,512]{3,2,1,0:T(8,128)(2,1)}) %tuple.42), branch_computations={%region_2.0_spmd, %region_3.0_spmd} | conditional | flops 2150629376 | bytes 39845952
  7.1 2.4 %fusion.36 = f32[2,512,512]{2,1,0:T(8,128)S(1)} fusion(bf16[2,2,512,512]{3,2,1,0:T(8,128)(2,1)} %get-tuple-element.53, bf16[2,2,512,512]{3,2,1,0:T(8,128)(2,1)} %get-tuple-element.52), kind=kOutput, calls=%fused_computation.45 | convolution fusion | flops 536870912 | bytes 4194304 | tf_op jit(solution)/shard_map/cond/branch_0_fun/bij,bjk->bik/dot_general | solution.py:34
  12.0 1.5 pad_maximum_fusion.2
  13.6 3.2 %copy.32 = bf16[2,2,8,64,512]{4,3,1,0,2:T(8,128)(2,1)} copy(bf16[2,2,8,64,512]{4,3,2,1,0:T(8,128)(2,1)} %bitcast.220) | data formatting | bytes 4194304 | tf_op jit(solution)/shard_map/reshape | solution.py:54
  16.7 7.3 %all-to-all-start = ((bf16[2,2,8,64,512]{4,3,1,0,2:T(8,128)(2,1)}), bf16[2,2,8,64,512]{4,3,1,0,2:T(8,128)(2,1)}, u32[]{:S(2)}, u32[]{:S(2)}) async-start(bf16[2,2,8,64,512]{4,3,1,0,2:T(8,128)(2,1)} %copy.32), calls=%async_computation | async-start | bytes 4194304 | tf_op jit(solution)/shard_map/all_to_all | solution.py:72
  24.7 4.5 %conditional.7 = (bf16[2,2,8,64,512]{4,3,2,1,0:T(8,128)(2,1)S(1)}) conditional(s32[]{:T(128)} %bitcast.38, (bf16[2,2,512,512]{3,2,1,0:T(8,128)(2,1)}, bf16[2,2,512,512]{3,2,1,0:T(8,128)(2,1)S(1)}) %tuple.39, (bf16[2,2,512,512]{3,2,1,0:T(8,128)(2,1)S(1)}, bf16[2,2,512,512]{3,2,1,0:T(8,128)(2,1)}) %tuple.40), branch_computations={%region_0.0_spmd, %region_1.0_spmd} | conditional | flops 2150629376 | bytes 31457316
  24.7 2.1 %fusion.24 = f32[2,512,512]{2,1,0:T(8,128)S(1)} fusion(bf16[2,2,512,512]{3,2,1,0:T(8,128)(2,1)} %get-tuple-element.51, bf16[2,2,512,512]{3,2,1,0:T(8,128)(2,1)S(1)} %get-tuple-element.50), kind=kOutput, calls=%fused_computation.30 | convolution fusion | flops 536870912 | bytes 4194304 | tf_op jit(solution)/shard_map/cond/branch_1_fun/bij,bjk->bik/dot_general | solution.py:31
  30.6 2.0 %collective-permute-start = (bf16[2,2,1,64,512]{4,3,2,1,0:T(8,128)(2,1)}, bf16[2,2,1,64,512]{4,3,2,1,0:T(8,128)(2,1)S(1)}, u32[]{:S(2)}, u32[]{:S(2)}) collective-permute-start(bf16[2,2,1,64,512]{4,3,2,1,0:T(8,128)(2,1)} %get-tuple-element.75), channel_id=1, source_target_pairs={{0,2},{2,0},{4,6},{6,4},{8,10},{10,8},{12,14},{14,12},{1,3},{3,1},... | collective-permute-start | bytes 786440 | tf_op jit(solution)/shard_map/ppermute | solution.py:18
  34.0 2.9 %collective-permute-start.3 = (bf16[2,2,1,64,512]{4,3,2,1,0:T(8,128)(2,1)}, bf16[2,2,1,64,512]{4,3,2,1,0:T(8,128)(2,1)S(1)}, u32[]{:S(2)}, u32[]{:S(2)}) collective-permute-start(bf16[2,2,1,64,512]{4,3,2,1,0:T(8,128)(2,1)} %get-tuple-element.72), channel_id=1, source_target_pairs={{0,8},{2,10},{4,12},{6,14},{8,0},{10,2},{12,4},{14,6},{1,9},{3,11}... | collective-permute-start | bytes 786440 | tf_op jit(solution)/shard_map/ppermute | solution.py:18
  40.3 7.7 %collective-permute-done = bf16[2,2,1,64,512]{4,3,2,1,0:T(8,128)(2,1)S(1)} collective-permute-done((bf16[2,2,1,64,512]{4,3,2,1,0:T(8,128)(2,1)}, bf16[2,2,1,64,512]{4,3,2,1,0:T(8,128)(2,1)S(1)}, u32[]{:S(2)}, u32[]{:S(2)}) %collective-permute-start) | collective-permute-done | bytes 262176 | tf_op jit(solution)/shard_map/ppermute | solution.py:18
  48.0 9.4 %collective-permute-start.5 = (bf16[2,2,1,64,512]{4,3,2,1,0:T(8,128)(2,1)}, bf16[2,2,1,64,512]{4,3,2,1,0:T(8,128)(2,1)S(1)}, u32[]{:S(2)}, u32[]{:S(2)}) collective-permute-start(bf16[2,2,1,64,512]{4,3,2,1,0:T(8,128)(2,1)} %get-tuple-element.70), channel_id=1, source_target_pairs={{0,12},{2,14},{4,8},{6,10},{8,4},{10,6},{12,0},{14,2},{1,13},{3,15... | collective-permute-start | bytes 786440 | tf_op jit(solution)/shard_map/ppermute | solution.py:18
  57.4 8.5 %collective-permute-done.1 = bf16[2,2,1,64,512]{4,3,2,1,0:T(8,128)(2,1)S(1)} collective-permute-done((bf16[2,2,1,64,512]{4,3,2,1,0:T(8,128)(2,1)}, bf16[2,2,1,64,512]{4,3,2,1,0:T(8,128)(2,1)S(1)}, u32[]{:S(2)}, u32[]{:S(2)}) %collective-permute-start.1) | collective-permute-done | bytes 262176 | tf_op jit(solution)/shard_map/ppermute | solution.py:18
  65.9 3.7 %collective-permute-start.6 = (bf16[2,2,1,64,512]{4,3,2,1,0:T(8,128)(2,1)}, bf16[2,2,1,64,512]{4,3,2,1,0:T(8,128)(2,1)S(1)}, u32[]{:S(2)}, u32[]{:S(2)}) collective-permute-start(bf16[2,2,1,64,512]{4,3,2,1,0:T(8,128)(2,1)} %get-tuple-element.69), channel_id=1, source_target_pairs={{0,14},{2,12},{4,10},{6,8},{8,6},{10,4},{12,2},{14,0},{1,15},{3,13... | collective-permute-start | bytes 786440 | tf_op jit(solution)/shard_map/ppermute | solution.py:18
  69.6 1.9 %collective-permute-done.2 = bf16[2,2,1,64,512]{4,3,2,1,0:T(8,128)(2,1)S(1)} collective-permute-done((bf16[2,2,1,64,512]{4,3,2,1,0:T(8,128)(2,1)}, bf16[2,2,1,64,512]{4,3,2,1,0:T(8,128)(2,1)S(1)}, u32[]{:S(2)}, u32[]{:S(2)}) %collective-permute-start.2) | collective-permute-done | bytes 262176 | tf_op jit(solution)/shard_map/ppermute | solution.py:18
  71.5 30.2 %collective-permute-done.3 = bf16[2,2,1,64,512]{4,3,2,1,0:T(8,128)(2,1)S(1)} collective-permute-done((bf16[2,2,1,64,512]{4,3,2,1,0:T(8,128)(2,1)}, bf16[2,2,1,64,512]{4,3,2,1,0:T(8,128)(2,1)S(1)}, u32[]{:S(2)}, u32[]{:S(2)}) %collective-permute-start.3) | collective-permute-done | bytes 262176 | tf_op jit(solution)/shard_map/ppermute | solution.py:18
  101.8 6.1 %collective-permute-done.4 = bf16[2,2,1,64,512]{4,3,2,1,0:T(8,128)(2,1)S(1)} collective-permute-done((bf16[2,2,1,64,512]{4,3,2,1,0:T(8,128)(2,1)}, bf16[2,2,1,64,512]{4,3,2,1,0:T(8,128)(2,1)S(1)}, u32[]{:S(2)}, u32[]{:S(2)}) %collective-permute-start.4) | collective-permute-done | bytes 262176 | tf_op jit(solution)/shard_map/ppermute | solution.py:18
  109.3 2.0 %copy.33 = bf16[2,2,8,64,512]{4,3,1,2,0:T(8,128)(2,1)S(1)} copy(bf16[2,2,8,64,512]{4,3,1,0,2:T(8,128)(2,1)} %all-to-all-done) | data formatting | bytes 4194304 | tf_op jit(solution)/shard_map/all_to_all | solution.py:72
  111.5 3.1 %conditional.18 = (bf16[2,2,512,512]{3,2,1,0:T(8,128)(2,1)S(1)}) conditional(s32[]{:T(128)} %bitcast.37, (bf16[2,2,512,512]{3,2,1,0:T(8,128)(2,1)S(1)}, bf16[2,2,512,512]{3,2,1,0:T(8,128)(2,1)S(1)}) %tuple.68, (bf16[2,2,512,512]{3,2,1,0:T(8,128)(2,1)S(1)}, bf16[2,2,512,512]{3,2,1,0:T(8,128)(2,1)S(1)}) %tuple.69), branch_computations={%region_4.0_spmd, %region_5.0_spmd} | conditional | flops 2150629376 | bytes 23068680
  114.8 61.0 %all_to_all.30 = bf16[2,2,8,64,512]{4,3,1,0,2:T(8,128)(2,1)S(1)} all-to-all(bf16[2,2,8,64,512]{4,3,1,0,2:T(8,128)(2,1)S(1)} %copy.34), channel_id=1, replica_groups=mesh['cuts'=2,'mode'=8,'branch'=2] {'mode'}, dimensions={2} | all-to-all | bytes 4194304 | tf_op jit(solution)/shard_map/all_to_all | solution.py:80
  176.8 1.7 slice_bitcast_fusion.9
  178.7 1.7 collective-permute-done.7
  180.4 2.0 %broadcast_select_fusion.3 = (bf16[2,2,512,512]{3,2,1,0:T(8,128)(2,1)S(1)}, bf16[2,2,512,512]{3,2,1,0:T(8,128)(2,1)S(1)}, bf16[2,2,512,512]{3,2,1,0:T(8,128)(2,1)S(1)}) fusion(pred[]{:T(512)} %bitcast.36, bf16[2,2,512,512]{3,2,1,0:T(8,128)(2,1)} %collective-permute-done.7, bf16[2,2,512,512]{3,2,1,0:T(8,128)(2,1)S(1)} %bitcast.224, pred[]{:T(512)S(6)} %eq.28), kind=kLoop, calls=%fused_computation.134 | loop fusion | flops 3145728 | bytes 10485762 | tf_op jit(solution)/shard_map/jit(_where)/select_n | solution.py:93
  186.2 1.5 pad_maximum_fusion.6
  (59 shorter events, 20.4 us)
Async XLA Ops:
  0.0 5.7 %copy-start.9 = (s32[7]{0:T(128)S(1)}, s32[7]{0:T(128)}, u32[]{:S(2)}) copy-start(s32[7]{0:T(128)} %param.11) | copy-start | bytes 88
  7.0 2.4 %copy-start.4 = (bf16[2,2,512,512]{3,2,1,0:T(8,128)(2,1)S(1)}, bf16[2,2,512,512]{3,2,1,0:T(8,128)(2,1)}, u32[]{:S(2)}) copy-start(bf16[2,2,512,512]{3,2,1,0:T(8,128)(2,1)} %get-tuple-element.53) | copy-start | bytes 6291460 | tf_op jit(solution)/shard_map/conditional
  7.1 2.8 %copy-start.6 = (bf16[2,2,512,512]{3,2,1,0:T(8,128)(2,1)S(1)}, bf16[2,2,512,512]{3,2,1,0:T(8,128)(2,1)}, u32[]{:S(2)}) copy-start(bf16[2,2,512,512]{3,2,1,0:T(8,128)(2,1)} %get-tuple-element.52) | copy-start | bytes 6291460 | tf_op jit(solution)/shard_map/conditional
  16.7 92.6 %all-to-all-start = ((bf16[2,2,8,64,512]{4,3,1,0,2:T(8,128)(2,1)}), bf16[2,2,8,64,512]{4,3,1,0,2:T(8,128)(2,1)}, u32[]{:S(2)}, u32[]{:S(2)}) async-start(bf16[2,2,8,64,512]{4,3,1,0,2:T(8,128)(2,1)} %copy.32), calls=%async_computation | async-start | bytes 4194304 | tf_op jit(solution)/shard_map/all_to_all | solution.py:72
  24.7 2.1 %copy-start.3 = (bf16[2,2,512,512]{3,2,1,0:T(8,128)(2,1)S(1)}, bf16[2,2,512,512]{3,2,1,0:T(8,128)(2,1)}, u32[]{:S(2)}) copy-start(bf16[2,2,512,512]{3,2,1,0:T(8,128)(2,1)} %get-tuple-element.51) | copy-start | bytes 6291460 | tf_op jit(solution)/shard_map/conditional.3
  29.1 9.3 %copy-start.8 = (bf16[2,2,8,64,512]{4,3,2,1,0:T(8,128)(2,1)}, bf16[2,2,8,64,512]{4,3,2,1,0:T(8,128)(2,1)S(1)}, u32[]{:S(2)}) copy-start(bf16[2,2,8,64,512]{4,3,2,1,0:T(8,128)(2,1)S(1)} %get-tuple-element.80) | copy-start | bytes 6291460
  30.6 17.4 %collective-permute-start = (bf16[2,2,1,64,512]{4,3,2,1,0:T(8,128)(2,1)}, bf16[2,2,1,64,512]{4,3,2,1,0:T(8,128)(2,1)S(1)}, u32[]{:S(2)}, u32[]{:S(2)}) collective-permute-start(bf16[2,2,1,64,512]{4,3,2,1,0:T(8,128)(2,1)} %get-tuple-element.75), channel_id=1, source_target_pairs={{0,2},{2,0},{4,6},{6,4},{8,10},{10,8},{12,14},{14,12},{1,3},{3,1},... | collective-permute-start | bytes 786440 | tf_op jit(solution)/shard_map/ppermute | solution.py:18
  32.6 33.3 %collective-permute-start.1 = (bf16[2,2,1,64,512]{4,3,2,1,0:T(8,128)(2,1)}, bf16[2,2,1,64,512]{4,3,2,1,0:T(8,128)(2,1)S(1)}, u32[]{:S(2)}, u32[]{:S(2)}) collective-permute-start(bf16[2,2,1,64,512]{4,3,2,1,0:T(8,128)(2,1)} %get-tuple-element.74), channel_id=1, source_target_pairs={{0,4},{2,6},{4,0},{6,2},{8,12},{10,14},{12,8},{14,10},{1,5},{3,7},... | collective-permute-start | bytes 786440 | tf_op jit(solution)/shard_map/ppermute | solution.py:18
  34.0 37.5 %collective-permute-start.2 = (bf16[2,2,1,64,512]{4,3,2,1,0:T(8,128)(2,1)}, bf16[2,2,1,64,512]{4,3,2,1,0:T(8,128)(2,1)S(1)}, u32[]{:S(2)}, u32[]{:S(2)}) collective-permute-start(bf16[2,2,1,64,512]{4,3,2,1,0:T(8,128)(2,1)} %get-tuple-element.73), channel_id=1, source_target_pairs={{0,6},{2,4},{4,2},{6,0},{8,14},{10,12},{12,10},{14,8},{1,7},{3,5},... | collective-permute-start | bytes 786440 | tf_op jit(solution)/shard_map/ppermute | solution.py:18
  34.0 67.7 %collective-permute-start.3 = (bf16[2,2,1,64,512]{4,3,2,1,0:T(8,128)(2,1)}, bf16[2,2,1,64,512]{4,3,2,1,0:T(8,128)(2,1)S(1)}, u32[]{:S(2)}, u32[]{:S(2)}) collective-permute-start(bf16[2,2,1,64,512]{4,3,2,1,0:T(8,128)(2,1)} %get-tuple-element.72), channel_id=1, source_target_pairs={{0,8},{2,10},{4,12},{6,14},{8,0},{10,2},{12,4},{14,6},{1,9},{3,11}... | collective-permute-start | bytes 786440 | tf_op jit(solution)/shard_map/ppermute | solution.py:18
  37.0 70.9 %collective-permute-start.4 = (bf16[2,2,1,64,512]{4,3,2,1,0:T(8,128)(2,1)}, bf16[2,2,1,64,512]{4,3,2,1,0:T(8,128)(2,1)S(1)}, u32[]{:S(2)}, u32[]{:S(2)}) collective-permute-start(bf16[2,2,1,64,512]{4,3,2,1,0:T(8,128)(2,1)} %get-tuple-element.71), channel_id=1, source_target_pairs={{0,10},{2,8},{4,14},{6,12},{8,2},{10,0},{12,6},{14,4},{1,11},{3,9}... | collective-permute-start | bytes 786440 | tf_op jit(solution)/shard_map/ppermute | solution.py:18
  48.0 59.9 %collective-permute-start.5 = (bf16[2,2,1,64,512]{4,3,2,1,0:T(8,128)(2,1)}, bf16[2,2,1,64,512]{4,3,2,1,0:T(8,128)(2,1)S(1)}, u32[]{:S(2)}, u32[]{:S(2)}) collective-permute-start(bf16[2,2,1,64,512]{4,3,2,1,0:T(8,128)(2,1)} %get-tuple-element.70), channel_id=1, source_target_pairs={{0,12},{2,14},{4,8},{6,10},{8,4},{10,6},{12,0},{14,2},{1,13},{3,15... | collective-permute-start | bytes 786440 | tf_op jit(solution)/shard_map/ppermute | solution.py:18
  65.9 42.1 %collective-permute-start.6 = (bf16[2,2,1,64,512]{4,3,2,1,0:T(8,128)(2,1)}, bf16[2,2,1,64,512]{4,3,2,1,0:T(8,128)(2,1)S(1)}, u32[]{:S(2)}, u32[]{:S(2)}) collective-permute-start(bf16[2,2,1,64,512]{4,3,2,1,0:T(8,128)(2,1)} %get-tuple-element.69), channel_id=1, source_target_pairs={{0,14},{2,12},{4,10},{6,8},{8,6},{10,4},{12,2},{14,0},{1,15},{3,13... | collective-permute-start | bytes 786440 | tf_op jit(solution)/shard_map/ppermute | solution.py:18
  108.0 1.3 copy-start
  109.3 2.2 %copy-start.1 = (bf16[2,16,1,64,512]{4,3,1,0,2:T(8,128)(2,1)S(1)}, bf16[2,16,1,64,512]{4,3,1,0,2:T(8,128)(2,1)}, u32[]{:S(2)}) copy-start(bf16[2,16,1,64,512]{4,3,1,0,2:T(8,128)(2,1)} %copy-done) | copy-start | bytes 6291460
  175.8 0.9 copy-start.10
  176.0 4.4 %collective-permute-start.7 = (bf16[2,2,512,512]{3,2,1,0:T(8,128)(2,1)S(1)}, bf16[2,2,512,512]{3,2,1,0:T(8,128)(2,1)}, u32[]{:S(2)}, u32[]{:S(2)}) collective-permute-start(bf16[2,2,512,512]{3,2,1,0:T(8,128)(2,1)S(1)} %bitcast.223), channel_id=1, source_target_pairs={{0,1},{1,0},{2,3},{3,2},{4,5},{5,4},{6,7},{7,6},{8,9},{9,8},{10,11... | collective-permute-start | bytes 6291464 | tf_op jit(solution)/shard_map/ppermute | solution.py:26
